TPU v7x, 256 devices: a whole 4x4x8 slice. The times are simulated.
256 devices in a mesh: users: 32 (over y, z_lo, core), heads: 8 (over x, z_hi).
Axes of the slice: x: 4, y: 4, z: 8 (z_hi: 2, z_lo: 4; z = z_hi * 4 + z_lo), core: 2. Of those that a mesh axis runs over, the one named last changes fastest.
Arguments:
- sessions: bfloat16 [65536, 4096], P(('users', 'heads')), parts along dimension 0, may hold values from -16 to 16
- input_weight: bfloat16 [3, 4096, 2048], P(None, None, 'heads'), may hold values from -1 to 1
- output_weight: bfloat16 [2048, 4096], P('heads'), may hold values from -0.359375 to 0.359375
- session_counts: int32 [64], P('users'), parts along dimension 0, may hold values from 1 to 1536, 2048 in all
Outputs:
- attended: bfloat16 [65536, 4096], P(('users', 'heads')), parts along dimension 0
There are 32 independent parts, one for each index of `users`. A program takes and returns all parts, laid end to end along the dimension named above; an argument that names none is the same for every part. Nothing has to cross between parts.
Inputs may be any that keep to these rules, and one draw needn't show every extreme that they name: `session_counts`: the 2 counts sum to 2048.
All inputs are finite; a program needn't handle non-finite values.
Results may differ from a plain program's by a relative error of at most 0.015.
Values may be sent and summed in bfloat16 or wider, within the bound.
A program may use at most 128 MiB of HBM per device.

v0:
```python
import jax
import jax.numpy as jnp
from jax import lax
from jax.sharding import PartitionSpec as P

HD = 128


def permitted(total, counts):
    positions = jnp.arange(total, dtype=jnp.int32)
    ends = jnp.cumsum(counts)
    row_user = jnp.sum((positions[:, None] >= ends[None, :]).astype(jnp.int32), axis=1)
    same_user = row_user[:, None] == row_user[None, :]
    return jnp.logical_and(same_user, positions[:, None] >= positions[None, :])


def attend(packed, allowed):
    total = packed.shape[1]
    width = packed.shape[2]
    block = min(512, total)
    count = total // block
    queries = packed[0].reshape(count, block, width // HD, HD)
    key_rows = packed[1].reshape(total, width // HD, HD)
    values = packed[2].reshape(total, width // HD, HD)
    masks = allowed.reshape(count, block, total)

    def one_block(pair):
        query_block, mask_block = pair
        scores = jnp.einsum(
            "qhe,khe->hqk", query_block, key_rows, preferred_element_type=jnp.float32
        ) * HD ** (-0.5)
        scores = jnp.where(mask_block[None], scores, -1e30)
        highest = jnp.max(scores, axis=2, keepdims=True)
        raised = jnp.where(mask_block[None], jnp.exp(scores - highest), 0.0)
        attn_probs = (raised / jnp.sum(raised, axis=2, keepdims=True)).astype(jnp.bfloat16)
        mixed = jnp.einsum("hqk,khe->qhe", attn_probs, values, preferred_element_type=jnp.float32)
        return mixed.astype(jnp.bfloat16).reshape(block, width)

    blocks_out = lax.map(one_block, (queries, masks))
    return blocks_out.reshape(total, width)


def per_device(sessions, input_weight, output_weight, session_counts):
    packed = jnp.einsum(
        "nd,cde->cne",
        lax.all_gather(sessions, "heads", axis=0, tiled=True),
        input_weight,
        preferred_element_type=jnp.float32,
    ).astype(jnp.bfloat16)
    total = packed.shape[1]
    allowed = permitted(total, session_counts)
    mixed = attend(packed, allowed)
    return lax.psum_scatter(
        jnp.dot(mixed, output_weight, preferred_element_type=jnp.float32).astype(jnp.bfloat16),
        "heads",
        scatter_dimension=0,
        tiled=True,
    )


def solution(mesh):
    in_specs = (P(("users", "heads"), None), P(None, None, "heads"), P("heads", None), P("users"))
    out_specs = P(("users", "heads"), None)
    return jax.shard_map(
        per_device, mesh=mesh, in_specs=in_specs, out_specs=out_specs, check_vma=False
    )
```

profile of v0, /device:TPU:14, one launch (start us, length us, event | category | flops | bytes accessed | tf_op | source)
XLA Modules:
  0.0 721.1 jit_solution(13063207499974208347)
XLA Ops:
  6.5 0.7 all-gather.2.cloned.1.call-update
  7.3 0.8 reduce-window.8
  8.3 5.8 fusion.28
  14.1 304.2 %all-gather.2.cloned.1.call-done = bf16[2048,4096]{1,0:T(8,128)(2,1)} async-done(((bf16[256,4096]{1,0:T(8,128)(2,1)}), bf16[2048,4096]{1,0:T(8,128)(2,1)}) %all-gather.2.cloned.1.call-update) | async-done | bytes 16777232 | tf_op jit(solution)/shard_map/all_gather | solution.py:46
  318.3 18.6 %fusion.32 = bf16[3,2048,256]{1,2,0:T(8,128)(2,1)S(1)} fusion(bf16[3,4096,256]{2,1,0:T(8,128)(2,1)} %param.7, bf16[2048,4096]{1,0:T(8,128)(2,1)} %all-gather.2.cloned.1.call-done), kind=kOutput, calls=%fused_computation.28 | convolution fusion | flops 12886474752 | bytes 26214400 | tf_op jit(solution)/shard_map/nd,cde->cne/dot_general | solution.py:44
  336.9 1.6 fusion.41
  338.5 1.3 copy.14
  339.8 1.8 reshape_squeeze.9
  341.7 1.7 copy.13
  343.4 63.7 %while.10 = (s32[]{:T(128)}, bf16[4,512,256]{2,1,0:T(8,128)(2,1)}, pred[4,512,2048]{2,1,0:T(8,128)(4,1)}, bf16[4,512,2,128]{3,1,2,0:T(8,128)(2,1)}, bf16[2048,2,...) while((s32[]{:T(128)}, bf16[4,512,256]{2,1,0:T(8,128)(2,1)}, ...), condition=%wide.region_5.6_spmd, body=%wide.region_2.5_spmd.sunk | while | flops 1088555008 | bytes 24649824 | solution.py:39
  343.4 1.3 dynamic-slice_bitcast_fusion.2
  344.7 8.6 %fusion.56 = (f32[2,512]{1,0:T(2,128)S(1)}, f32[2,512,2048]{2,1,0:T(8,128)}) fusion(pred[512,2048]{1,0:T(8,128)(4,1)S(1)} %dynamic-slice_bitcast_fusion.2, bf16[2048,2,128]{2,0,1:T(8,128)(2,1)} %get-tuple-element.132, bf16[4,512,2,128]{3,1,2,0:T(8,128)(2,1)} %get-tuple-element.131, s32[]{:T(128)S(6)} %copy.24), kind=kOutput, calls=%fused_computation.32.clone.1 | convolution fusion | flops 547358720 | bytes 11800580 | tf_op jit(solution)/shard_map/while/body/eval_jaxpr/sub | solution.py:34
  353.2 5.2 fusion.57
  358.4 0.1 copy.20
  358.6 0.7 constant_dynamic-update-slice_fusion.2
  359.3 1.3 dynamic-slice_bitcast_fusion.2
  360.6 8.6 %fusion.56 = (f32[2,512]{1,0:T(2,128)S(1)}, f32[2,512,2048]{2,1,0:T(8,128)}) fusion(pred[512,2048]{1,0:T(8,128)(4,1)S(1)} %dynamic-slice_bitcast_fusion.2, bf16[2048,2,128]{2,0,1:T(8,128)(2,1)} %get-tuple-element.132, bf16[4,512,2,128]{3,1,2,0:T(8,128)(2,1)} %get-tuple-element.131, s32[]{:T(128)S(6)} %copy.24), kind=kOutput, calls=%fused_computation.32.clone.1 | convolution fusion | flops 547358720 | bytes 11800580 | tf_op jit(solution)/shard_map/while/body/eval_jaxpr/sub | solution.py:34
  369.2 5.2 fusion.57
  374.4 0.1 copy.20
  374.5 0.7 constant_dynamic-update-slice_fusion.2
  375.2 1.3 dynamic-slice_bitcast_fusion.2
  376.5 8.6 %fusion.56 = (f32[2,512]{1,0:T(2,128)S(1)}, f32[2,512,2048]{2,1,0:T(8,128)}) fusion(pred[512,2048]{1,0:T(8,128)(4,1)S(1)} %dynamic-slice_bitcast_fusion.2, bf16[2048,2,128]{2,0,1:T(8,128)(2,1)} %get-tuple-element.132, bf16[4,512,2,128]{3,1,2,0:T(8,128)(2,1)} %get-tuple-element.131, s32[]{:T(128)S(6)} %copy.24), kind=kOutput, calls=%fused_computation.32.clone.1 | convolution fusion | flops 547358720 | bytes 11800580 | tf_op jit(solution)/shard_map/while/body/eval_jaxpr/sub | solution.py:34
  385.1 5.2 fusion.57
  390.3 0.1 copy.20
  390.4 0.7 constant_dynamic-update-slice_fusion.2
  391.2 1.3 dynamic-slice_bitcast_fusion.2
  392.5 8.6 %fusion.56 = (f32[2,512]{1,0:T(2,128)S(1)}, f32[2,512,2048]{2,1,0:T(8,128)}) fusion(pred[512,2048]{1,0:T(8,128)(4,1)S(1)} %dynamic-slice_bitcast_fusion.2, bf16[2048,2,128]{2,0,1:T(8,128)(2,1)} %get-tuple-element.132, bf16[4,512,2,128]{3,1,2,0:T(8,128)(2,1)} %get-tuple-element.131, s32[]{:T(128)S(6)} %copy.24), kind=kOutput, calls=%fused_computation.32.clone.1 | convolution fusion | flops 547358720 | bytes 11800580 | tf_op jit(solution)/shard_map/while/body/eval_jaxpr/sub | solution.py:34
  401.0 5.2 fusion.57
  406.2 0.1 copy.20
  406.4 0.7 constant_dynamic-update-slice_fusion.2
  407.1 9.3 %convolution_convert_fusion = bf16[2048,4096]{1,0:T(8,128)(2,1)} fusion(bf16[2048,256]{1,0:T(8,128)(2,1)} %bitcast.52, bf16[256,4096]{1,0:T(8,128)(2,1)S(1)} %copy-done), kind=kOutput, calls=%fused_computation.26 | convolution fusion | flops 4303355904 | bytes 19922944 | tf_op jit(solution)/shard_map/dot_general | solution.py:54
  416.4 297.8 %reduce-scatter.2.cloned.1.call-done = bf16[256,4096]{1,0:T(8,128)(2,1)} async-done(((bf16[2048,4096]{1,0:T(8,128)(2,1)}), bf16[256,4096]{1,0:T(8,128)(2,1)}) %reduce-scatter.2.cloned.1.call-update) | async-done | bytes 2097168 | tf_op jit(solution)/shard_map/reduce_scatter | solution.py:53
  (9 shorter events, 0.2 us)
Async XLA Ops:
  6.5 400.6 %copy-start = (bf16[256,4096]{1,0:T(8,128)(2,1)S(1)}, bf16[256,4096]{1,0:T(8,128)(2,1)}, u32[]{:S(2)}) copy-start(bf16[256,4096]{1,0:T(8,128)(2,1)} %param.8) | copy-start | bytes 6291460
  6.5 311.8 %all-gather.2.cloned.1.call-start = ((), (), s32[]{:S(2)}) async-start(), calls=%async_computation.1 | async-start | bytes 18874368 | tf_op jit(solution)/shard_map/all_gather | solution.py:46
  7.3 707.0 %reduce-scatter.2.cloned.1.call-start = ((), (), s32[]{:S(2)}) async-start(), calls=%async_computation.2 | async-start | bytes 18874368 | tf_op jit(solution)/shard_map/reduce_scatter | solution.py:53
Sparse Core Ops, SparseCore 0:
  10.0 308.2 all-gather.1
  416.5 297.6 reduce-scatter.1
where the time goes:
time: 733 us; the launch traced here: 721 us
  waiting for transfers between devices  603 us (82%)
  matrix products  82.9 us (11%)
  local copies, waits for them, and re-layouts  15.1 us (2%)
  between operations  13.4 us (2%)
    all_gather x1, waiting for transfers between devices, per_device(): lax.all_gather(sessions, 'heads', axis=0, tiled=True)  304 us
    reduce_scatter x1, waiting for transfers between devices, per_device(): lax.psum_scatter(jnp.dot(mixed, output_weight, preferred_element_type=jnp...  298 us
    sub x4, matrix products, one_block(): raised = jnp.where(mask_block[None], jnp.exp(scores - highest), 0.0)  34.2 us
    dot_general x4, matrix products, one_block(): jnp.einsum('hqk,khe->qhe', attn_probs, values, preferred_element_type=jnp...  20.8 us
    dot_general x1, matrix products, per_device(): jnp.einsum('nd,cde->cne', lax.all_gather(sessions, 'heads', axis=0, tiled...  18.6 us
  transfers between devices with their start and end apart: 2, of which 2 were waited for; matrix products, arithmetic and copies ran while one was open for 1% of the time, Pallas kernels for 0%

commit v1 on v0

v1 whole, which is shorter than its diff:
```python
import jax
import jax.numpy as jnp
from jax import lax
from jax.experimental import pallas as pl
from jax.experimental.pallas import tpu as pltpu
from jax.sharding import PartitionSpec as P

HD = 128
D = 4096
ROWS = 256
HALF = 128
TOTAL = 2048
COLS = 256
MESH = pl.DeviceIdType.MESH

ZX = 0
R1P, R1M = 2, 4
R2P, R2M = 6, 7
SX = 8
WZ = 16
WYP, WYM, WY2 = 20, 23, 26
WXP, WXM, WX2 = 29, 30, 31
V1P, V1M = 32, 34
V2P, V2M = 36, 37
SV = 38
CN = 46
NCOPY = 47


def place(x, y, z, c):
    x, y, z, c = (lax.rem(x + 4, 4), lax.rem(y + 4, 4), lax.rem(z + 8, 8), lax.rem(c, 2))
    return ((y * 4 + lax.rem(z, 4)) * 2 + c, x * 2 + z // 4)


def kernel(
    cnt_ref, x_hbm, w_hbm, v_hbm, out_hbm,
    xg, wq, vg, qkv, obuf, mix, obf, cnt,
    ssem, rsem, osend, orecv, lsem, outsem,
):
    u, h = lax.axis_index("users"), lax.axis_index("heads")
    x, s, y, zl, c = h // 2, lax.rem(h, 2), u // 8, lax.rem(u // 2, 4), lax.rem(u, 2)
    z = s * 4 + zl
    native = c == s
    foreign = c != s
    edge = jnp.logical_or(zl == 0, zl == 3)
    dz_out = jnp.where(zl >= 2, 1, 7)
    dz_in = jnp.where(zl >= 2, 7, 1)
    xm, xp, x2 = lax.rem(x + 3, 4), lax.rem(x + 1, 4), lax.rem(x + 2, 4)
    ym, yp, y2 = lax.rem(y + 3, 4), lax.rem(y + 1, 4), lax.rem(y + 2, 4)
    sib = place(x, y, z, c + 1)
    to_xp, to_xm, to_x2 = place(xp, y, z, c), place(xm, y, z, c), place(x2, y, z, c)
    to_yp, to_ym, to_y2 = place(x, yp, z, c), place(x, ym, z, c), place(x, y2, z, c)
    across = place(x, y, z + 4, c + 1)
    outer = place(x, y, z + dz_out, c)
    inner = place(x, y, z + dz_in, c)

    def copy(i, src, dst, target):
        return pltpu.make_async_remote_copy(
            src_ref=src, dst_ref=dst, send_sem=ssem.at[i], recv_sem=rsem.at[i],
            device_id=target, device_id_type=MESH,
        )

    def send(i, ref, target):
        copy(i, ref, ref, target).start()

    def got(i, ref):
        copy(i, ref, ref, sib).wait_recv()

    def sent(i, ref):
        copy(i, ref, ref, sib).wait_send()

    def xh(bx, bp, half):
        return xg.at[bx, bp, half]

    def vlo(by):
        return vg.at[pl.ds(0, 2), c, by]

    def vhi(by):
        return vg.at[pl.ds(2, 2), c, by]

    def wpart(ref, m):
        return ref.at[m, pl.ds(pl.multiple_of(y * 1024, 1024), 1024)]

    vmine = vg.at[x, c, y]
    quarter = v_hbm.at[pl.ds(pl.multiple_of(y * 64, 64), 64)]

    load_x = [
        pltpu.make_async_copy(x_hbm.at[pl.ds(HALF * i, HALF)], xh(x, c, i), lsem.at[i])
        for i in range(2)
    ]
    load_w = pltpu.make_async_copy(w_hbm, wq, lsem.at[2])
    load_v = pltpu.make_async_copy(quarter, vmine, lsem.at[3])

    @pl.when(native)
    def _():
        load_v.start()
        for cp in load_x:
            cp.start()
        load_w.start()
        cnt[...] = jnp.full(cnt.shape, cnt_ref[0], jnp.int32)

    barrier = pltpu.get_barrier_semaphore()
    peers = [place(x + dx, y, z + dz, c + dc) for dx in range(4) for dz in (0, 4) for dc in (0, 1)][1:]
    peers += [to_yp, to_ym, to_y2, place(x, y, z + 1, c), place(x, y, z + 7, c)]
    for peer in peers:
        pl.semaphore_signal(barrier, inc=1, device_id=peer, device_id_type=MESH)
    pl.semaphore_wait(barrier, len(peers))

    def share_v():
        send(WXP, vmine, to_xp)
        send(WXM, vmine, to_xm)
        send(WX2, vmine, to_x2)

    def first_a():
        send(R1P, xh(x, c, 0), to_xp)
        send(R1M, xh(x, c, 0), to_xm)
        send(SX, xh(x, c, 0), sib)

    def first_b():
        send(R1P + 1, xh(x, c, 1), to_xp)
        send(R1M + 1, xh(x, c, 1), to_xm)
        send(SX + 1, xh(x, c, 1), sib)

    def bundle():
        for i in (WXP, WXM, WX2):
            got(i, vmine)
        send(V1P, vlo(y), to_yp)
        send(V1M + 1, vhi(y), to_ym)
        send(V1P + 1, vhi(y), to_yp)
        send(V1M, vlo(y), to_ym)
        send(SV, vlo(y), sib)
        send(SV + 1, vhi(y), sib)

    def bundle_on():
        got(V1P, vlo(ym))
        send(V2P, vlo(ym), to_yp)
        send(SV + 2, vlo(ym), sib)
        got(V1M + 1, vhi(yp))
        send(V2M, vhi(yp), to_ym)
        send(SV + 5, vhi(yp), sib)
        got(V1P + 1, vhi(ym))
        send(SV + 3, vhi(ym), sib)
        got(V1M, vlo(yp))
        send(SV + 4, vlo(yp), sib)

    @pl.when(native)
    def _():
        @pl.when(edge)
        def _():
            copy(WZ + 3, quarter, vmine, outer).start()
            for m in range(3):
                copy(WZ + m, wpart(w_hbm, m), wpart(wq, m), outer).start()

        send(CN, cnt, sib)
        load_v.wait()
        share_v()
        for cp in load_x:
            cp.wait()
        first_a()
        first_b()
        bundle()

    @pl.when(foreign)
    def _():
        for i in range(2):
            copy(ZX + i, x_hbm.at[pl.ds(HALF * i, HALF)], xh(x, 1 - c, i), across).start()

        def relay(i, ref):
            got(i, ref)

            @pl.when(edge)
            def _():
                send(i, ref, inner)

        def spread(m):
            relay(WZ + m, wpart(wq, m))
            send(WYP + m, wpart(wq, m), to_yp)
            send(WYM + m, wpart(wq, m), to_ym)
            send(WY2 + m, wpart(wq, m), to_y2)

        relay(WZ + 3, vmine)
        share_v()
        spread(0)
        got(ZX, xh(x, c, 0))
        first_a()
        spread(1)
        spread(2)
        got(ZX + 1, xh(x, c, 1))
        first_b()

    got(R1P, xh(xm, c, 0))
    send(R2P, xh(xm, c, 0), to_xp)
    send(SX + 2, xh(xm, c, 0), sib)
    got(R1M + 1, xh(xp, c, 1))
    send(R2M, xh(xp, c, 1), to_xm)
    send(SX + 5, xh(xp, c, 1), sib)
    got(R1P + 1, xh(xm, c, 1))
    send(SX + 3, xh(xm, c, 1), sib)
    got(R1M, xh(xp, c, 0))
    send(SX + 4, xh(xp, c, 0), sib)

    @pl.when(native)
    def _():
        load_w.wait()

    @pl.when(foreign)
    def _():
        bundle()
        got(CN, cnt)
        for i in (WYP, WYM, WY2):
            for m in range(3):
                got(i + m, wpart(wq, m))

    def step(k, carry):
        @pl.when(k == 3)
        def _():
            got(SX, xh(x, 1 - c, 0))
            got(SX + 1, xh(x, 1 - c, 1))

            @pl.when(native)
            def _():
                bundle_on()

        @pl.when(k == 4)
        def _():
            got(SX + 2, xh(xm, 1 - c, 0))
            got(SX + 3, xh(xm, 1 - c, 1))

        @pl.when(k == 5)
        def _():
            got(SX + 4, xh(xp, 1 - c, 0))
            got(SX + 5, xh(xp, 1 - c, 1))

        @pl.when(k == 6)
        def _():
            got(R2P, xh(x2, c, 0))
            send(SX + 6, xh(x2, c, 0), sib)
            got(R2M, xh(x2, c, 1))
            send(SX + 7, xh(x2, c, 1), sib)

        @pl.when(k == 7)
        def _():
            got(SX + 6, xh(x2, 1 - c, 0))
            got(SX + 7, xh(x2, 1 - c, 1))

        last = k // 6
        r = lax.rem(k, 3)
        dx = (1 - last) * (r * 3 - (r // 2) * 5) + last * 2
        dp = (1 - last) * (k // 3) + last * (k - 6)
        bx, bp = lax.rem(x + dx, 4), lax.rem(c + dp, 2)
        rows = xg[bx, bp].reshape(ROWS, D)
        at = pl.ds(pl.multiple_of((bx * 2 + bp) * ROWS, ROWS), ROWS)
        for m in range(3):
            qkv[m, at, :] = jnp.dot(rows, wq[m], preferred_element_type=jnp.float32).astype(jnp.bfloat16)
        return carry

    lax.fori_loop(0, 8, step, 0)

    @pl.when(foreign)
    def _():
        bundle_on()

    mine = x * 2 + c
    start = cnt[0:1, 0:1]
    scale = HD**-0.5
    for i in range(8):
        width = (i + 1) * ROWS
        row = i * ROWS + lax.broadcasted_iota(jnp.int32, (ROWS, 1), 0)
        col = lax.broadcasted_iota(jnp.int32, (ROWS, width), 1)
        low = jnp.where(row >= start, start, 0)
        allowed = jnp.logical_and(col >= low, col <= row)
        for hd in range(2):
            lanes = slice(hd * HD, (hd + 1) * HD)
            q = qkv[0, i * ROWS : width, lanes]
            scores = lax.dot_general(
                q, qkv[1, :width, lanes], (((1,), (1,)), ((), ())), preferred_element_type=jnp.float32
            )
            scores = jnp.where(allowed, scores, -1e30)
            highest = jnp.max(scores, axis=1, keepdims=True)
            raised = jnp.exp((scores - highest) * scale)
            total = jnp.sum(raised, axis=1, keepdims=True)
            o = jnp.dot(raised.astype(jnp.bfloat16), qkv[2, :width, lanes], preferred_element_type=jnp.float32)
            obuf[i, :, lanes] = (o / total).astype(jnp.bfloat16)
        bx, bz = i // 2, i % 2
        home = jnp.logical_and(jnp.logical_and(x == bx, s == bz), native)
        owner = place(bx, y, bz * 4 + zl, s)

        @pl.when(home)
        def _():
            mix[mine] = obuf[i]

        @pl.when(jnp.logical_not(home))
        def _():
            pltpu.make_async_remote_copy(
                src_ref=obuf.at[i], dst_ref=mix.at[mine], send_sem=osend.at[i], recv_sem=orecv.at[mine],
                device_id=owner, device_id_type=MESH,
            ).start()

    got(V2P, vlo(y2))
    send(SV + 6, vlo(y2), sib)
    got(V2M, vhi(y2))
    send(SV + 7, vhi(y2), sib)
    for by, i in ((y, 0), (ym, 2), (yp, 4), (y2, 6)):
        got(SV + i, vg.at[pl.ds(0, 2), 1 - c, by])
        got(SV + i + 1, vg.at[pl.ds(2, 2), 1 - c, by])

    for g in range(8):
        here = jnp.logical_and(native, mine == g)

        @pl.when(jnp.logical_not(here))
        def _():
            pltpu.make_async_remote_copy(
                src_ref=mix.at[g], dst_ref=mix.at[g], send_sem=osend.at[0], recv_sem=orecv.at[g],
                device_id=sib, device_id_type=MESH,
            ).wait_recv()

    mixed = jnp.concatenate([mix[g] for g in range(8)], axis=1)
    chunk = 512

    def store(n):
        at = pl.ds(pl.multiple_of(n * chunk, chunk), chunk)
        return pltpu.make_async_copy(obf.at[:, at], out_hbm.at[:, at], outsem.at[n])

    def project(n, carry):
        at = pl.ds(pl.multiple_of(n * chunk, chunk), chunk)
        weight = vg[:, :, :, :, at].reshape(TOTAL, chunk)
        obf[:, at] = jnp.dot(mixed, weight, preferred_element_type=jnp.float32).astype(jnp.bfloat16)
        store(n).start()
        return carry

    lax.fori_loop(0, D // chunk, project, 0)

    for i in range(2):
        for j in (R1P, R1M, SX, SX + 2, SX + 4, SX + 6):
            sent(j + i, xh(x, c, i))
        for j in (V1P, V1M, SV, SV + 2, SV + 4, SV + 6):
            sent(j + i, vlo(y))
    for j in (R2P, R2M):
        sent(j, xh(x, c, 0))
    for j in (V2P, V2M):
        sent(j, vlo(y))
    for j in (WXP, WXM, WX2):
        sent(j, vmine)

    @pl.when(native)
    def _():
        sent(CN, cnt)

    @pl.when(foreign)
    def _():
        for i in range(2):
            sent(ZX + i, xh(x, c, i))
        for j in (WYP, WYM, WY2):
            for m in range(3):
                sent(j + m, wpart(wq, m))

    @pl.when(edge)
    def _():
        for m in range(3):
            sent(WZ + m, wpart(wq, m))
        sent(WZ + 3, vmine)

    for i in range(8):
        bx, bz = i // 2, i % 2
        home = jnp.logical_and(jnp.logical_and(x == bx, s == bz), native)

        @pl.when(jnp.logical_not(home))
        def _():
            pltpu.make_async_remote_copy(
                src_ref=obuf.at[i], dst_ref=mix.at[i], send_sem=osend.at[i], recv_sem=orecv.at[i],
                device_id=sib, device_id_type=MESH,
            ).wait_send()

    for n in range(D // chunk):
        store(n).wait()


def per_device(sessions, input_weight, output_weight, session_counts):
    return pl.pallas_call(
        kernel,
        out_shape=jax.ShapeDtypeStruct((ROWS, D), jnp.bfloat16),
        in_specs=[pl.BlockSpec(memory_space=pltpu.SMEM)] + [pl.BlockSpec(memory_space=pl.ANY)] * 3,
        out_specs=pl.BlockSpec(memory_space=pl.ANY),
        scratch_shapes=[
            pltpu.VMEM((4, 2, 2, HALF, D), jnp.bfloat16),
            pltpu.VMEM((3, D, COLS), jnp.bfloat16),
            pltpu.VMEM((4, 2, 4, 64, D), jnp.bfloat16),
            pltpu.VMEM((3, TOTAL, COLS), jnp.bfloat16),
            pltpu.VMEM((8, ROWS, COLS), jnp.bfloat16),
            pltpu.VMEM((8, ROWS, COLS), jnp.bfloat16),
            pltpu.VMEM((ROWS, D), jnp.bfloat16),
            pltpu.VMEM((8, 128), jnp.int32),
            pltpu.SemaphoreType.DMA((NCOPY,)),
            pltpu.SemaphoreType.DMA((NCOPY,)),
            pltpu.SemaphoreType.DMA((8,)),
            pltpu.SemaphoreType.DMA((8,)),
            pltpu.SemaphoreType.DMA((4,)),
            pltpu.SemaphoreType.DMA((8,)),
        ],
        compiler_params=pltpu.CompilerParams(
            collective_id=0, has_side_effects=True, vmem_limit_bytes=60 * 2**20
        ),
        name="layer",
    )(session_counts, sessions, input_weight, output_weight)


def solution(mesh):
    in_specs = (P(("users", "heads"), None), P(None, None, "heads"), P("heads", None), P("users"))
    out_specs = P(("users", "heads"), None)
    return jax.shard_map(
        per_device, mesh=mesh, in_specs=in_specs, out_specs=out_specs, check_vma=False
    )
```

time: 733 us -> 178 us (0.24)
  the two profiles are of different devices: /device:TPU:14 before, /device:TPU:39 now
where the time goes in v1:
time: 178 us
  Pallas kernels  175 us (98%)
  local copies, waits for them, and re-layouts  3.13 us (2%)
    pallas_call x1, Pallas kernels, per_device(): pl.pallas_call(kernel, out_shape=jax.ShapeDtypeStruct((ROWS, D), jnp.bflo...  175 us

profile of v1, /device:TPU:39, one launch (start us, length us, event | category | flops | bytes accessed | tf_op | source)
XLA Modules:
  0.0 177.8 jit_solution(3560783766880252630)
XLA Ops:
  0.0 174.6 %layer.1 = bf16[256,4096]{1,0:T(8,128)(2,1)} custom-call(s32[2]{0:T(128)} %cnt_ref.1, bf16[256,4096]{1,0:T(8,128)(2,1)} %x_hbm.1, bf16[3,4096,256]{2,1,0:T(8,128)(2,1)} %w_hbm.1, bf16[256,4096]{1,0:T(8,128)(2,1)} %v_hbm.1), custom_call_target="tpu_custom_call" | custom-call | tf_op jit(solution)/shard_map/layer/pallas_call | solution.py:379
  174.6 3.1 %copy.6 = bf16[256,4096]{1,0:T(8,128)(2,1)} copy(bf16[256,4096]{1,0:T(8,128)(2,1)} %layer.1) | data formatting | bytes 4194304

commit v2 on v1

v2 whole, which is shorter than its diff:
```python
import jax
import jax.numpy as jnp
from jax import lax
from jax.experimental import pallas as pl
from jax.experimental.pallas import tpu as pltpu
from jax.sharding import PartitionSpec as P

HD = 128
D = 4096
ROWS = 256
CHUNK = 64
TOTAL = 2048
COLS = 256
MESH = pl.DeviceIdType.MESH
ORDER = (0, 2, 1, 3)

ZX = 0
R1P, R1M = 4, 8
R2 = 12
SX = 16
WZ = 80
W1P, W1M = 88, 94
W2P, W2M = 32, 35
VXP, VXM, VX2 = 46, 47, 48
V1P, V1M = 49, 53
V2P, V2M = 57, 60
SV = 63
CN = 79
SW = 100
VF = 112
VX3 = 113
NCOPY = 114


def place(x, y, z, c):
    x, y, z, c = (lax.rem(x + 4, 4), lax.rem(y + 4, 4), lax.rem(z + 8, 8), lax.rem(c, 2))
    return ((y * 4 + lax.rem(z, 4)) * 2 + c, x * 2 + z // 4)


def kernel(
    cnt_ref, x_hbm, w_hbm, v_hbm, out_hbm,
    xg, wq, wf, vg, qkv, obuf, mix, obf, cnt,
    ssem, rsem, osend, orecv, lsem, outsem,
):
    u, h = lax.axis_index("users"), lax.axis_index("heads")
    x, s, y, zl, c = h // 2, lax.rem(h, 2), u // 8, lax.rem(u // 2, 4), lax.rem(u, 2)
    z = s * 4 + zl
    native = c == s
    foreign = c != s
    xm, xp, x2 = lax.rem(x + 3, 4), lax.rem(x + 1, 4), lax.rem(x + 2, 4)
    ym, yp, y2 = lax.rem(y + 3, 4), lax.rem(y + 1, 4), lax.rem(y + 2, 4)
    sib = place(x, y, z, c + 1)
    to_xp, to_xm, to_x2 = place(xp, y, z, c), place(xm, y, z, c), place(x2, y, z, c)
    to_yp, to_ym = place(x, yp, z, c), place(x, ym, z, c)
    across = place(x, y, z + 4, c + 1)
    up, down = place(x, y, z + 1, c), place(x, y, z + 7, c)
    border = place(x, y, z + jnp.where(zl == 3, 1, 7), c + 1)

    def copy(i, src, dst, target):
        return pltpu.make_async_remote_copy(
            src_ref=src, dst_ref=dst, send_sem=ssem.at[i], recv_sem=rsem.at[i],
            device_id=target, device_id_type=MESH,
        )

    def send(i, ref, target):
        copy(i, ref, ref, target).start()

    def got(i, ref):
        copy(i, ref, ref, sib).wait_recv()

    def sent(i, ref):
        copy(i, ref, ref, sib).wait_send()

    def xc(p, j, bx):
        return xg.at[p, j, bx]

    def wp(m, by, ref=None):
        return (wf if ref is None else ref).at[m, pl.ds(pl.multiple_of(by * 1024, 1024), 1024)]

    def wh(m, by, half):
        return wf.at[m, pl.ds(pl.multiple_of(by * 1024 + half * 512, 512), 512)]

    def vp(bx, by):
        return vg.at[bx, c, by]

    def vh(bx, by, half):
        return vg.at[bx, c, by, pl.ds(half * 32, 32)]

    vmine = vp(x, y)
    quarter = v_hbm.at[pl.ds(pl.multiple_of(y * CHUNK, CHUNK), CHUNK)]

    load_x = [
        pltpu.make_async_copy(x_hbm.at[pl.ds(CHUNK * j, CHUNK)], xc(c, j, x), lsem.at[j]) for j in range(4)
    ]
    load_v = [
        pltpu.make_async_copy(v_hbm.at[pl.ds(CHUNK * j, CHUNK)], vg.at[x, s, j], lsem.at[4 + j])
        for j in range(4)
    ]
    load_w = pltpu.make_async_copy(w_hbm, wq, lsem.at[8])

    @pl.when(native)
    def _():
        for cp in load_x:
            cp.start()
        cnt[...] = jnp.full(cnt.shape, cnt_ref[0], jnp.int32)

    for cp in load_v:
        cp.start()

    @pl.when(native)
    def _():
        load_w.start()

    barrier = pltpu.get_barrier_semaphore()
    peers = [place(x + dx, y, z + dz, c + dc) for dx in range(4) for dz in (0, 4) for dc in (0, 1)][1:]
    peers += [to_yp, to_ym, up, down, place(x, y, z + 1, c + 1), place(x, y, z + 7, c + 1)]
    for peer in peers:
        pl.semaphore_signal(barrier, inc=1, device_id=peer, device_id_type=MESH)
    pl.semaphore_wait(barrier, len(peers))

    def first(j):
        send(R1P + j, xc(c, j, x), to_xp)
        send(R1M + j, xc(c, j, x), to_xm)
        send(SX + j, xc(c, j, x), sib)

    def ring(j):
        got(R1P + j, xc(c, j, xm))
        if j < 2:
            send(R2 + j, xc(c, j, xm), to_xp)
        send(SX + 4 + j, xc(c, j, xm), sib)
        got(R1M + j, xc(c, j, xp))
        if j >= 2:
            send(R2 + j, xc(c, j, xp), to_xm)
        send(SX + 8 + j, xc(c, j, xp), sib)

    def tail(j):
        got(R2 + j, xc(c, j, x2))
        send(SX + 12 + j, xc(c, j, x2), sib)

    def from_sib(j):
        for i, bx in enumerate((x, xm, xp, x2)):
            got(SX + 4 * i + j, xc(1 - c, j, bx))

    def share_v():
        send(VXP, vmine, to_xp)
        send(VXM, vmine, to_xm)

    def along_y(q, bx):
        send(V1P + q, vp(bx, y), to_yp)
        send(V1M + q, vp(bx, y), to_ym)
        if q:
            send(SV + q, vp(bx, y), sib)

    def gather_v():
        got(VXP, vp(xm, y))
        send(VX2, vh(xm, y, 0), to_xp)
        along_y(1, xm)
        got(VXM, vp(xp, y))
        send(VX3, vh(xp, y, 1), to_xm)
        along_y(2, xp)

    def gather_v2():
        got(VX2, vh(x2, y, 0))
        got(VX3, vh(x2, y, 1))
        along_y(3, x2)

    def forward_v(own):
        for q, bx in ((1, xm), (2, xp), (3, x2)) + (((0, x),) if own else ()):
            got(V1P + q, vp(bx, ym))
            if q == 1:
                send(V2P, vp(bx, ym), to_yp)
            if q in (0, 3):
                send(V2P + 1 + q // 3, vh(bx, ym, 0), to_yp)
            send(SV + 4 + q, vp(bx, ym), sib)
            got(V1M + q, vp(bx, yp))
            if q == 2:
                send(V2M, vp(bx, yp), to_ym)
            if q in (0, 3):
                send(V2M + 1 + q // 3, vh(bx, yp, 1), to_ym)
            send(SV + 8 + q, vp(bx, yp), sib)

    def last_v(own):
        got(V2P, vp(xm, y2))
        send(SV + 12 + 1, vp(xm, y2), sib)
        got(V2M, vp(xp, y2))
        send(SV + 12 + 2, vp(xp, y2), sib)
        for q, bx in ((3, x2),) + (((0, x),) if own else ()):
            got(V2P + 1 + q // 3, vh(bx, y2, 0))
            got(V2M + 1 + q // 3, vh(bx, y2, 1))
            send(SV + 12 + q, vp(bx, y2), sib)

    def across_z(j):
        copy(ZX + j, x_hbm.at[pl.ds(CHUNK * j, CHUNK)], xc(1 - c, j, x), across).start()

    def piece(m, half):
        return vg.at[x, 1 - c, y, pl.ds(half * 32, 32)] if m == 3 else wh(m, y, half)

    near = zl // 2
    near_to, far_to = place(x, y, z + 9 - 2 * near, c), place(x, y, z + 7 + 2 * near, c)

    def along(m, half):
        if m < 3:
            send(W1P + 2 * m + half, wh(m, y, half), to_yp)
            send(W1M + 2 * m + half, wh(m, y, half), to_ym)

    def relay_near(m):
        i, ref = WZ + 4 * near + m, piece(m, near)
        got(i, ref)
        send(i, ref, near_to)
        along(m, near)

    def relay_far(m):
        i, ref = WZ + 4 * (1 - near) + m, piece(m, 1 - near)
        got(i, ref)

        @pl.when(jnp.logical_or(zl == 1, zl == 2))
        def _():
            send(i, ref, far_to)

        along(m, 1 - near)

    def hand_out(i):
        got(ZX + ORDER[i], xc(c, ORDER[i], x))
        first(ORDER[i])

    def over_border(m, half, i, target):
        if m == 3:
            src = v_hbm.at[pl.ds(pl.multiple_of(y * CHUNK + half * 32, 32), 32)]
            return copy(i + m, src, vh(x, y, half), target)
        src = w_hbm.at[m, pl.ds(pl.multiple_of(y * 1024 + half * 512, 512), 512)]
        return copy(i + m, src, piece(m, half), target)

    def weight_to_sib(i, m, by):
        copy(SW + 3 * i + m, wp(m, by), wp(m, by, wq), sib).start()

    def weights_on(m):
        for half in range(2):
            i = 2 * m + half
            got(W1P + i, wh(m, ym, half))
            if i < 3:
                send(W2P + i, wh(m, ym, half), to_yp)
            got(W1M + i, wh(m, yp, half))
            if i >= 3:
                send(W2M + i - 3, wh(m, yp, half), to_ym)
        weight_to_sib(1, m, ym)
        weight_to_sib(2, m, yp)

    def weights_last():
        for i in range(6):
            got((W2P if i < 3 else W2M - 3) + i, wh(i // 2, y2, i % 2))
            if i % 2:
                weight_to_sib(3, i // 2, y2)

    @pl.when(native)
    def _():
        for edge, half, i in ((3, 0, WZ), (0, 1, WZ + 4)):

            @pl.when(zl == edge)
            def _():
                over_border(0, half, i, border).start()
                over_border(1, half, i, border).start()

        send(CN, cnt, sib)
        for cp in load_x:
            cp.wait()
        for cp in load_v:
            cp.wait()
        share_v()
        for j in ORDER:
            first(j)
        for edge, half, i in ((3, 0, WZ), (0, 1, WZ + 4)):

            @pl.when(zl == edge)
            def _():
                for m in (2, 3):
                    over_border(m - 2, half, i, border).wait_send()
                    over_border(m, half, i, border).start()

        for m in range(4):
            relay_near(m)
        for m in range(4):
            relay_far(m)
        send(VF, vg.at[x, 1 - c, y], sib)
        for m in range(3):
            weight_to_sib(0, m, y)
        gather_v()
        for j in ORDER:
            ring(j)
        for m in range(3):
            weights_on(m)
        gather_v2()
        for j in ORDER:
            tail(j)
        weights_last()
        load_w.wait()

    @pl.when(foreign)
    def _():
        got(VF, vmine)
        across_z(ORDER[0])
        across_z(ORDER[1])
        got(CN, cnt)
        share_v()
        along_y(0, x)
        hand_out(0)
        across_z(ORDER[2])
        gather_v()
        hand_out(1)
        across_z(ORDER[3])
        ring(ORDER[0])
        gather_v2()
        hand_out(2)
        ring(ORDER[1])
        for cp in load_v:
            cp.wait()
        for i, by in enumerate((y, ym, yp, y2)):
            for m in range(3):
                got(SW + 3 * i + m, wp(m, by, wq))

    def step(k, carry):
        for i, j in enumerate(ORDER):

            @pl.when(k == i)
            def _():
                @pl.when(native)
                def _():
                    if i == 3:
                        forward_v(False)

                @pl.when(foreign)
                def _():
                    from_sib(j)
                    if i == 1:
                        hand_out(3)
                        ring(ORDER[2])

            @pl.when(k == 4 + i)
            def _():
                @pl.when(native)
                def _():
                    from_sib(j)

                @pl.when(foreign)
                def _():
                    if i == 2:
                        ring(ORDER[3])
                    tail(j)

        second, r = k // 4, lax.rem(k, 4)
        p = lax.rem(s + second, 2)
        j = (r // 2) + 2 * lax.rem(r, 2)
        rows = xg[p, j].reshape(ROWS, D)
        for m in range(3):
            done = jnp.dot(rows, wq[m], preferred_element_type=jnp.float32).astype(jnp.bfloat16)
            for bx in range(4):
                at = pl.ds(pl.multiple_of((bx * 2 + p) * ROWS + j * CHUNK, CHUNK), CHUNK)
                qkv[m, at, :] = done[bx * CHUNK : (bx + 1) * CHUNK]
        return carry

    lax.fori_loop(0, 8, step, 0)

    @pl.when(foreign)
    def _():
        forward_v(True)

    mine = x * 2 + c
    start = cnt[0:1, 0:1]
    scale = HD**-0.5
    for i in range(8):
        width = (i + 1) * ROWS
        row = i * ROWS + lax.broadcasted_iota(jnp.int32, (ROWS, 1), 0)
        col = lax.broadcasted_iota(jnp.int32, (ROWS, width), 1)
        low = jnp.where(row >= start, start, 0)
        allowed = jnp.logical_and(col >= low, col <= row)
        for hd in range(2):
            lanes = slice(hd * HD, (hd + 1) * HD)
            q = qkv[0, i * ROWS : width, lanes]
            scores = lax.dot_general(
                q, qkv[1, :width, lanes], (((1,), (1,)), ((), ())), preferred_element_type=jnp.float32
            )
            scores = jnp.where(allowed, scores, -1e30)
            highest = jnp.max(scores, axis=1, keepdims=True)
            raised = jnp.exp((scores - highest) * scale)
            total = jnp.sum(raised, axis=1, keepdims=True)
            o = jnp.dot(raised.astype(jnp.bfloat16), qkv[2, :width, lanes], preferred_element_type=jnp.float32)
            obuf[i, :, lanes] = (o / total).astype(jnp.bfloat16)
        bx, bz = i // 2, i % 2
        home = jnp.logical_and(jnp.logical_and(x == bx, s == bz), native)
        owner = place(bx, y, bz * 4 + zl, s)

        @pl.when(home)
        def _():
            mix[mine] = obuf[i]

        @pl.when(jnp.logical_not(home))
        def _():
            pltpu.make_async_remote_copy(
                src_ref=obuf.at[i], dst_ref=mix.at[mine], send_sem=osend.at[i], recv_sem=orecv.at[mine],
                device_id=owner, device_id_type=MESH,
            ).start()

    @pl.when(native)
    def _():
        last_v(False)

    @pl.when(foreign)
    def _():
        last_v(True)

    for i, by in enumerate((y, ym, yp, y2)):
        for q, bx in ((1, xm), (2, xp), (3, x2)):
            got(SV + 4 * i + q, vg.at[bx, 1 - c, by])

        if i:

            @pl.when(native)
            def _():
                got(SV + 4 * i, vg.at[x, 1 - c, by])

    for g in range(8):
        here = jnp.logical_and(native, mine == g)

        @pl.when(jnp.logical_not(here))
        def _():
            pltpu.make_async_remote_copy(
                src_ref=mix.at[g], dst_ref=mix.at[g], send_sem=osend.at[0], recv_sem=orecv.at[g],
                device_id=sib, device_id_type=MESH,
            ).wait_recv()

    mixed = jnp.concatenate([mix[g] for g in range(8)], axis=1)
    chunk = 512

    def store(n):
        at = pl.ds(pl.multiple_of(n * chunk, chunk), chunk)
        return pltpu.make_async_copy(obf.at[:, at], out_hbm.at[:, at], outsem.at[n])

    def project(n, carry):
        at = pl.ds(pl.multiple_of(n * chunk, chunk), chunk)
        weight = vg[:, :, :, :, at].reshape(TOTAL, chunk)
        obf[:, at] = jnp.dot(mixed, weight, preferred_element_type=jnp.float32).astype(jnp.bfloat16)
        store(n).start()
        return carry

    lax.fori_loop(0, D // chunk, project, 0)

    for i in range(4):
        for j in (R1P, R1M, R2, SX, SX + 4, SX + 8, SX + 12):
            sent(j + i, xc(c, i, x))
    for i in range(1, 4):
        for j in (V1P, V1M, SV, SV + 4, SV + 8, SV + 12):
            sent(j + i, vmine)
    for j in (VXP, VXM, V2P, V2M):
        sent(j, vmine)
    for j in (VX2, VX3):
        sent(j, vh(x, y, 0))
    for j in (V2P, V2M):
        sent(j + 2, vh(x, y, 0))

    @pl.when(native)
    def _():
        sent(CN, cnt)
        sent(VF, vmine)
        for i in range(6):
            for j in (W1P, W1M, W2P):
                sent(j + i, wh(0, y, 0))
        for i in range(12):
            sent(SW + i, wp(0, y))
        for m in range(4):
            sent(WZ + 4 * near + m, piece(m, near))

        @pl.when(jnp.logical_or(zl == 1, zl == 2))
        def _():
            for m in range(4):
                sent(WZ + 4 * (1 - near) + m, piece(m, 1 - near))

    @pl.when(foreign)
    def _():
        for i in range(4):
            sent(ZX + i, xc(c, i, x))
        for j in (V1P, V1M, SV + 4, SV + 8, SV + 12):
            sent(j, vmine)
        for j in (V2P, V2M):
            sent(j + 1, vh(x, y, 0))

    for edge, half, i in ((3, 0, WZ), (0, 1, WZ + 4)):

        @pl.when(jnp.logical_and(native, zl == edge))
        def _():
            for m in (2, 3):
                over_border(m, half, i, border).wait_send()

    for i in range(8):
        bx, bz = i // 2, i % 2
        home = jnp.logical_and(jnp.logical_and(x == bx, s == bz), native)

        @pl.when(jnp.logical_not(home))
        def _():
            pltpu.make_async_remote_copy(
                src_ref=obuf.at[i], dst_ref=mix.at[i], send_sem=osend.at[i], recv_sem=orecv.at[i],
                device_id=sib, device_id_type=MESH,
            ).wait_send()

    for n in range(D // chunk):
        store(n).wait()


def per_device(sessions, input_weight, output_weight, session_counts):
    return pl.pallas_call(
        kernel,
        out_shape=jax.ShapeDtypeStruct((ROWS, D), jnp.bfloat16),
        in_specs=[pl.BlockSpec(memory_space=pltpu.SMEM)] + [pl.BlockSpec(memory_space=pl.ANY)] * 3,
        out_specs=pl.BlockSpec(memory_space=pl.ANY),
        scratch_shapes=[
            pltpu.VMEM((2, 4, 4, CHUNK, D), jnp.bfloat16),
            pltpu.VMEM((3, D, COLS), jnp.bfloat16),
            pltpu.VMEM((3, D, COLS), jnp.bfloat16),
            pltpu.VMEM((4, 2, 4, CHUNK, D), jnp.bfloat16),
            pltpu.VMEM((3, TOTAL, COLS), jnp.bfloat16),
            pltpu.VMEM((8, ROWS, COLS), jnp.bfloat16),
            pltpu.VMEM((8, ROWS, COLS), jnp.bfloat16),
            pltpu.VMEM((ROWS, D), jnp.bfloat16),
            pltpu.VMEM((8, 128), jnp.int32),
            pltpu.SemaphoreType.DMA((NCOPY,)),
            pltpu.SemaphoreType.DMA((NCOPY,)),
            pltpu.SemaphoreType.DMA((8,)),
            pltpu.SemaphoreType.DMA((8,)),
            pltpu.SemaphoreType.DMA((9,)),
            pltpu.SemaphoreType.DMA((8,)),
        ],
        compiler_params=pltpu.CompilerParams(
            collective_id=0, has_side_effects=True, vmem_limit_bytes=60 * 2**20
        ),
        name="layer",
    )(session_counts, sessions, input_weight, output_weight)


def solution(mesh):
    in_specs = (P(("users", "heads"), None), P(None, None, "heads"), P("heads", None), P("users"))
    out_specs = P(("users", "heads"), None)
    return jax.shard_map(
        per_device, mesh=mesh, in_specs=in_specs, out_specs=out_specs, check_vma=False
    )
```

time: 178 us -> 155 us (0.87)
  the two profiles are of different devices: /device:TPU:39 before, /device:TPU:14 now
where the time goes in v2:
time: 155 us
  Pallas kernels  152 us (98%)
  local copies, waits for them, and re-layouts  3.13 us (2%)
    pallas_call x1, Pallas kernels, per_device(): pl.pallas_call(kernel, out_shape=jax.ShapeDtypeStruct((ROWS, D), jnp.bflo...  152 us
    unnamed x1, local copies, waits for them, and re-layouts  3.13 us

profile of v2, /device:TPU:14, one launch (start us, length us, event | category | flops | bytes accessed | tf_op | source)
XLA Modules:
  0.0 154.8 jit_solution(17942285563269975084)
XLA Ops:
  0.0 151.6 %layer.1 = bf16[256,4096]{1,0:T(8,128)(2,1)} custom-call(s32[2]{0:T(128)} %cnt_ref.1, bf16[256,4096]{1,0:T(8,128)(2,1)} %x_hbm.1, bf16[3,4096,256]{2,1,0:T(8,128)(2,1)} %w_hbm.1, bf16[256,4096]{1,0:T(8,128)(2,1)} %v_hbm.1), custom_call_target="tpu_custom_call" | custom-call | tf_op jit(solution)/shard_map/layer/pallas_call | solution.py:508
  151.7 3.1 %copy.6 = bf16[256,4096]{1,0:T(8,128)(2,1)} copy(bf16[256,4096]{1,0:T(8,128)(2,1)} %layer.1) | data formatting | bytes 4194304

commit v3 on v2

--- a/solution.py
+++ b/solution.py
@@ -284,13 +284,18 @@
         for m in range(3):
             weight_to_sib(0, m, y)
         gather_v()
-        for j in ORDER:
-            ring(j)
-        for m in range(3):
-            weights_on(m)
+        ring(ORDER[0])
+        ring(ORDER[1])
+        ring(ORDER[2])
+        ring(ORDER[3])
+        weights_on(0)
+        weights_on(1)
+        weights_on(2)
         gather_v2()
-        for j in ORDER:
-            tail(j)
+        tail(ORDER[0])
+        tail(ORDER[1])
+        tail(ORDER[2])
+        tail(ORDER[3])
         weights_last()
         load_w.wait()
 
@@ -302,13 +307,13 @@
         got(CN, cnt)
         share_v()
         along_y(0, x)
+        gather_v()
         hand_out(0)
         across_z(ORDER[2])
-        gather_v()
         hand_out(1)
         across_z(ORDER[3])
+        gather_v2()
         ring(ORDER[0])
-        gather_v2()
         hand_out(2)
         ring(ORDER[1])
         for cp in load_v:
@@ -342,7 +347,7 @@
 
                 @pl.when(foreign)
                 def _():
-                    if i == 2:
+                    if i == 0:
                         ring(ORDER[3])
                     tail(j)
 
@@ -365,7 +370,7 @@
 
     mine = x * 2 + c
     start = cnt[0:1, 0:1]
-    scale = HD**-0.5
+    scale = HD**-0.5 * 1.4426950408889634
     for i in range(8):
         width = (i + 1) * ROWS
         row = i * ROWS + lax.broadcasted_iota(jnp.int32, (ROWS, 1), 0)
@@ -380,7 +385,7 @@
             )
             scores = jnp.where(allowed, scores, -1e30)
             highest = jnp.max(scores, axis=1, keepdims=True)
-            raised = jnp.exp((scores - highest) * scale)
+            raised = jnp.exp2((scores - highest) * scale)
             total = jnp.sum(raised, axis=1, keepdims=True)
             o = jnp.dot(raised.astype(jnp.bfloat16), qkv[2, :width, lanes], preferred_element_type=jnp.float32)
             obuf[i, :, lanes] = (o / total).astype(jnp.bfloat16)
@@ -441,7 +446,7 @@
         store(n).start()
         return carry
 
-    lax.fori_loop(0, D // chunk, project, 0)
+    lax.fori_loop(0, D // chunk, project, 0, unroll=True)
 
     for i in range(4):
         for j in (R1P, R1M, R2, SX, SX + 4, SX + 8, SX + 12):

time: 155 us -> 149 us (0.961)
  Pallas kernels: 152 us -> 146 us
    pallas_call x1, Pallas kernels: 152 us -> 146 us  [per_device(): pl.pallas_call(kernel, out_shape=jax.ShapeDtypeStruct((ROWS, D), jnp.bflo...]
where the time goes in v3:
time: 149 us
  Pallas kernels  146 us (98%)
  local copies, waits for them, and re-layouts  3.13 us (2%)
    pallas_call x1, Pallas kernels, per_device(): pl.pallas_call(kernel, out_shape=jax.ShapeDtypeStruct((ROWS, D), jnp.bflo...  146 us
    unnamed x1, local copies, waits for them, and re-layouts  3.13 us

profile of v3, /device:TPU:14, one launch (start us, length us, event | category | flops | bytes accessed | tf_op | source)
XLA Modules:
  0.0 149.2 jit_solution(4752543150325318135)
XLA Ops:
  0.0 146.0 %layer.1 = bf16[256,4096]{1,0:T(8,128)(2,1)} custom-call(s32[2]{0:T(128)} %cnt_ref.1, bf16[256,4096]{1,0:T(8,128)(2,1)} %x_hbm.1, bf16[3,4096,256]{2,1,0:T(8,128)(2,1)} %w_hbm.1, bf16[256,4096]{1,0:T(8,128)(2,1)} %v_hbm.1), custom_call_target="tpu_custom_call" | custom-call | tf_op jit(solution)/shard_map/layer/pallas_call | solution.py:513
  146.0 3.1 %copy.6 = bf16[256,4096]{1,0:T(8,128)(2,1)} copy(bf16[256,4096]{1,0:T(8,128)(2,1)} %layer.1) | data formatting | bytes 4194304
